TPU v7x, 32 devices: a whole 2x2x4 slice. The times are simulated.
32 devices in a mesh: rep: 16 (over z, x, core), shard: 2 (over y).
Axes of the slice: x: 2, y: 2, z: 4, core: 2. Of those that a mesh axis runs over, the one named last changes fastest.
Arguments:
- patches: bfloat16 [16384, 1280], P(('rep', 'shard')), may hold values from -6 to 6
- lengths: int32 [32, 4], P(('rep', 'shard')), may hold values from 1 to 256, 512 in all within a row
- positions: int32 [2, 16384], P(None, ('rep', 'shard')), may hold values from 0 to 63
- ln1_gain: bfloat16 [1280], P('shard'), may hold values from 0.5 to 1.5
- ln1_bias: bfloat16 [1280], P('shard'), may hold values from -3 to 3
- qkv_weight: bfloat16 [1280, 3840], P('shard'), may hold values from -0.15625 to 0.15625
- qkv_bias: bfloat16 [3840], P('shard'), may hold values from -3 to 3
- proj_weight: bfloat16 [1280, 1280], P('shard'), may hold values from -1.25 to 1.25
- proj_bias: bfloat16 [1280], P('shard'), may hold values from -3 to 3
- ln2_gain: bfloat16 [1280], P('shard'), may hold values from 0.5 to 1.5
- ln2_bias: bfloat16 [1280], P('shard'), may hold values from -3 to 3
- fc1_weight: bfloat16 [1280, 5120], P('shard'), may hold values from -0.15625 to 0.15625
- fc1_bias: bfloat16 [5120], P('shard'), may hold values from -3 to 3
- fc2_weight: bfloat16 [5120, 1280], P('shard'), may hold values from -0.125 to 0.125
- fc2_bias: bfloat16 [1280], P('shard'), may hold values from -3 to 3
- cotangent: bfloat16 [16384, 1280], P(('rep', 'shard')), may hold values from -6 to 6
Outputs:
- layer_out: bfloat16 [16384, 1280], P(('rep', 'shard'))
- d_patches: float32 [16384, 1280], P(('rep', 'shard'))
- d_ln1_gain: float32 [1280], P('shard')
- d_ln1_bias: float32 [1280], P('shard')
- d_qkv_weight: float32 [1280, 3840], P('shard')
- d_qkv_bias: float32 [3840], P('shard')
- d_proj_weight: float32 [1280, 1280], P('shard')
- d_proj_bias: float32 [1280], P('shard')
- d_ln2_gain: float32 [1280], P('shard')
- d_ln2_bias: float32 [1280], P('shard')
- d_fc1_weight: float32 [1280, 5120], P('shard')
- d_fc1_bias: float32 [5120], P('shard')
- d_fc2_weight: float32 [5120, 1280], P('shard')
- d_fc2_bias: float32 [1280], P('shard')
Inputs may be any that keep to these rules, and one draw needn't show every extreme that they name: `lengths`: each row's entries sum to 512; its largest entry is 256.
All inputs are finite; a program needn't handle non-finite values.
Results may differ from a plain program's by a relative error of at most 0.012.
The roundings to bfloat16 on the way count: a program that leaves them out, or rounds other values in their place, can miss the bound.
Values may be sent and summed in bfloat16 or wider, within the bound.
A program may use at most 320 MiB of HBM per device.

v0:
```python
from functools import partial
import jax
import jax.numpy as jnp
from jax import lax
from jax.sharding import PartitionSpec as P

HEADS = 16
norm_eps = 1e-06
quick_slope = 1.702


def apply_layer_norm(matrix):
    center = matrix - jnp.mean(matrix, axis=-1, keepdims=True)
    spread = jnp.mean(center * center, axis=-1, keepdims=True)
    inverse_spread = lax.rsqrt(spread + norm_eps)
    return (center * inverse_spread, inverse_spread)


def norm_gradient_step(normalized_gradient, centered_standard, inverse_spread, norm_gain):
    scaled_rows = normalized_gradient * norm_gain
    return inverse_spread * (
        scaled_rows
        - jnp.mean(scaled_rows, axis=-1, keepdims=True)
        - centered_standard * jnp.mean(scaled_rows * centered_standard, axis=-1, keepdims=True)
    )


def rotary_tables(positions, head_size):
    quarter = head_size // 4
    counter = jnp.arange(quarter, dtype=jnp.float32)
    inverse = jnp.power(jnp.float32(10000.0), -2.0 * counter / (head_size // 2))
    row_angle = positions[0].astype(jnp.float32)[:, None] * inverse[None, :]
    col_angle = positions[1].astype(jnp.float32)[:, None] * inverse[None, :]
    angle = jnp.concatenate([row_angle, col_angle], axis=1)
    angle = jnp.concatenate([angle, angle], axis=1)
    return (jnp.cos(angle), jnp.sin(angle))


def apply_rotary(matrix, cosine, sine):
    half_size = matrix.shape[-1] // 2
    turned = jnp.concatenate([-matrix[..., half_size:], matrix[..., :half_size]], axis=-1)
    return matrix * cosine[:, None, :] + turned * sine[:, None, :]


def rotary_back(grad_rows, cosine, sine):
    half_size = grad_rows.shape[-1] // 2
    sined = grad_rows * sine[:, None, :]
    turned = jnp.concatenate([sined[..., half_size:], -sined[..., :half_size]], axis=-1)
    return grad_rows * cosine[:, None, :] + turned


def masked_scores(queries, keys_rot, ident, score_scale):
    scores = (
        jnp.einsum("qhd,khd->hqk", queries, keys_rot, preferred_element_type=jnp.float32)
        * score_scale
    )
    same_pic = ident[:, None] == ident[None, :]
    return jnp.where(same_pic[None], scores, -1000000000.0)


def attend(pieces, score_scale):
    queries, keys_rot, values_all, ident = pieces
    scores = masked_scores(queries, keys_rot, ident, score_scale)
    top_score = jnp.max(scores, axis=2, keepdims=True)
    exp_scores = jnp.exp(scores - top_score)
    total = jnp.sum(exp_scores, axis=2, keepdims=True)
    probs = (exp_scores / total).astype(jnp.bfloat16)
    attended = jnp.einsum("hqk,khd->qhd", probs, values_all, preferred_element_type=jnp.float32)
    return (attended, (top_score + jnp.log(total))[:, :, 0])


def attend_back(pieces, score_scale):
    queries, keys_rot, values_all, ident, grad_heads, log_total = pieces
    scores = masked_scores(queries, keys_rot, ident, score_scale)
    probs = jnp.exp(scores - log_total[:, :, None])
    grad_probs = jnp.einsum(
        "qhd,khd->hqk", grad_heads, values_all, preferred_element_type=jnp.float32
    )
    inner = jnp.sum(probs * grad_probs, axis=2, keepdims=True)
    grad_scores = (probs * (grad_probs - inner)).astype(jnp.bfloat16)
    grad_query = (
        jnp.einsum("hqk,khd->qhd", grad_scores, keys_rot, preferred_element_type=jnp.float32)
        * score_scale
    )
    grad_key = (
        jnp.einsum("hqk,qhd->khd", grad_scores, queries, preferred_element_type=jnp.float32)
        * score_scale
    )
    grad_value = jnp.einsum(
        "hqk,qhd->khd", probs.astype(jnp.bfloat16), grad_heads, preferred_element_type=jnp.float32
    )
    return (grad_query, grad_key, grad_value)


def row_product(left, right):
    return jnp.einsum("ti,tj->ij", left, right, preferred_element_type=jnp.float32)


def back_product(grad_rows, weight_full):
    return jnp.einsum("tj,ij->ti", grad_rows, weight_full, preferred_element_type=jnp.float32)


def per_device(
    patches,
    lengths,
    positions,
    ln1_gain,
    ln1_bias,
    qkv_weight,
    qkv_bias,
    proj_weight,
    proj_bias,
    ln2_gain,
    ln2_bias,
    fc1_weight,
    fc1_bias,
    fc2_weight,
    fc2_bias,
    cotangent,
):
    pack_count = lengths.shape[0]
    row_count = patches.shape[0]
    length = row_count // pack_count
    model_width = patches.shape[1]
    head_count = HEADS
    head_size = model_width // head_count
    score_scale = head_size ** (-0.5)
    pic_ends = jnp.cumsum(lengths[:, :-1], axis=1)
    slot_index = jnp.arange(length, dtype=jnp.int32)
    idents = jnp.sum((slot_index[None, :, None] >= pic_ends[:, None, :]).astype(jnp.int32), axis=2)
    cosine, sine = rotary_tables(positions, head_size)
    pack_shape = (pack_count, length, head_count, head_size)
    first_norm_gain, first_norm_bias, w_qkv, b_qkv, w_proj, b_proj = (
        lax.all_gather(ln1_gain, "shard", axis=0, tiled=True),
        lax.all_gather(ln1_bias, "shard", axis=0, tiled=True),
        lax.all_gather(qkv_weight, "shard", axis=0, tiled=True),
        lax.all_gather(qkv_bias, "shard", axis=0, tiled=True),
        lax.all_gather(proj_weight, "shard", axis=0, tiled=True),
        lax.all_gather(proj_bias, "shard", axis=0, tiled=True),
    )
    input_rows = patches.astype(jnp.float32)
    first_centered_standard, first_inverse_spread = apply_layer_norm(input_rows)
    first_normalized = (
        first_centered_standard * first_norm_gain.astype(jnp.float32)
        + first_norm_bias.astype(jnp.float32)
    ).astype(jnp.bfloat16)
    qkv_rows = jnp.dot(first_normalized, w_qkv, preferred_element_type=jnp.float32) + b_qkv.astype(
        jnp.float32
    )
    qkv_rows = qkv_rows.reshape(row_count, 3, head_count, head_size)
    queries = apply_rotary(qkv_rows[:, 0], cosine, sine).astype(jnp.bfloat16).reshape(pack_shape)
    keys_rot = apply_rotary(qkv_rows[:, 1], cosine, sine).astype(jnp.bfloat16).reshape(pack_shape)
    values_all = qkv_rows[:, 2].astype(jnp.bfloat16).reshape(pack_shape)
    attended, log_total = lax.map(
        partial(attend, score_scale=score_scale), (queries, keys_rot, values_all, idents)
    )
    heads_out = attended.reshape(row_count, model_width).astype(jnp.bfloat16)
    hidden_rows = (
        input_rows
        + jnp.dot(heads_out, w_proj, preferred_element_type=jnp.float32)
        + b_proj.astype(jnp.float32)
    )
    second_norm_gain, second_norm_bias, w_up, b_up, w_down, b_down = (
        lax.all_gather(ln2_gain, "shard", axis=0, tiled=True),
        lax.all_gather(ln2_bias, "shard", axis=0, tiled=True),
        lax.all_gather(fc1_weight, "shard", axis=0, tiled=True),
        lax.all_gather(fc1_bias, "shard", axis=0, tiled=True),
        lax.all_gather(fc2_weight, "shard", axis=0, tiled=True),
        lax.all_gather(fc2_bias, "shard", axis=0, tiled=True),
    )
    second_centered_standard, second_inverse_spread = apply_layer_norm(hidden_rows)
    second_normalized = (
        second_centered_standard * second_norm_gain.astype(jnp.float32)
        + second_norm_bias.astype(jnp.float32)
    ).astype(jnp.bfloat16)
    up_pre = jnp.dot(second_normalized, w_up, preferred_element_type=jnp.float32) + b_up.astype(
        jnp.float32
    )
    sigmoid_up = 1.0 / (1.0 + jnp.exp(-quick_slope * up_pre))
    activation = (up_pre * sigmoid_up).astype(jnp.bfloat16)
    out_full = (
        hidden_rows
        + jnp.dot(activation, w_down, preferred_element_type=jnp.float32)
        + b_down.astype(jnp.float32)
    )
    layer_out = out_full.astype(jnp.bfloat16)
    second_norm_gain, second_norm_bias, w_up, b_up, w_down, b_down = (
        lax.all_gather(ln2_gain, "shard", axis=0, tiled=True),
        lax.all_gather(ln2_bias, "shard", axis=0, tiled=True),
        lax.all_gather(fc1_weight, "shard", axis=0, tiled=True),
        lax.all_gather(fc1_bias, "shard", axis=0, tiled=True),
        lax.all_gather(fc2_weight, "shard", axis=0, tiled=True),
        lax.all_gather(fc2_bias, "shard", axis=0, tiled=True),
    )
    grad_out = cotangent.astype(jnp.float32)
    d_w_down = row_product(activation, cotangent)
    d_b_down = jnp.sum(grad_out, axis=0)
    grad_act = back_product(cotangent, w_down)
    slope_up = sigmoid_up + quick_slope * up_pre * sigmoid_up * (1.0 - sigmoid_up)
    grad_pre = (grad_act * slope_up).astype(jnp.bfloat16)
    d_w_up = row_product(second_normalized, grad_pre)
    d_b_up = jnp.sum(grad_pre.astype(jnp.float32), axis=0)
    second_normalized_gradient = back_product(grad_pre, w_up)
    second_gain_gradient = jnp.sum(second_normalized_gradient * second_centered_standard, axis=0)
    d_bias_two = jnp.sum(second_normalized_gradient, axis=0)
    grad_hidden = grad_out + norm_gradient_step(
        second_normalized_gradient,
        second_centered_standard,
        second_inverse_spread,
        second_norm_gain.astype(jnp.float32),
    )
    m_gain, m_bias, m_up, m_upb, m_down, m_downb = (
        lax.psum_scatter(second_gain_gradient, "shard", scatter_dimension=0, tiled=True),
        lax.psum_scatter(d_bias_two, "shard", scatter_dimension=0, tiled=True),
        lax.psum_scatter(d_w_up, "shard", scatter_dimension=0, tiled=True),
        lax.psum_scatter(d_b_up, "shard", scatter_dimension=0, tiled=True),
        lax.psum_scatter(d_w_down, "shard", scatter_dimension=0, tiled=True),
        lax.psum_scatter(d_b_down, "shard", scatter_dimension=0, tiled=True),
    )
    m_gain, m_bias, m_up, m_upb, m_down, m_downb = lax.psum(
        (m_gain, m_bias, m_up, m_upb, m_down, m_downb), "rep"
    )
    first_norm_gain, first_norm_bias, w_qkv, b_qkv, w_proj, b_proj = (
        lax.all_gather(ln1_gain, "shard", axis=0, tiled=True),
        lax.all_gather(ln1_bias, "shard", axis=0, tiled=True),
        lax.all_gather(qkv_weight, "shard", axis=0, tiled=True),
        lax.all_gather(qkv_bias, "shard", axis=0, tiled=True),
        lax.all_gather(proj_weight, "shard", axis=0, tiled=True),
        lax.all_gather(proj_bias, "shard", axis=0, tiled=True),
    )
    grad_branch = grad_hidden.astype(jnp.bfloat16)
    d_w_proj = row_product(heads_out, grad_branch)
    d_b_proj = jnp.sum(grad_branch.astype(jnp.float32), axis=0)
    grad_heads = back_product(grad_branch, w_proj).astype(jnp.bfloat16).reshape(pack_shape)
    grad_query, grad_key, grad_value = lax.map(
        partial(attend_back, score_scale=score_scale),
        (queries, keys_rot, values_all, idents, grad_heads, log_total),
    )
    rows_shape = (row_count, head_count, head_size)
    grad_query = rotary_back(grad_query.reshape(rows_shape), cosine, sine)
    grad_key = rotary_back(grad_key.reshape(rows_shape), cosine, sine)
    grad_qkv = (
        jnp.stack([grad_query, grad_key, grad_value.reshape(rows_shape)], axis=1)
        .reshape(row_count, 3 * model_width)
        .astype(jnp.bfloat16)
    )
    d_w_qkv = row_product(first_normalized, grad_qkv)
    d_b_qkv = jnp.sum(grad_qkv.astype(jnp.float32), axis=0)
    first_normalized_gradient = back_product(grad_qkv, w_qkv)
    first_gain_gradient = jnp.sum(first_normalized_gradient * first_centered_standard, axis=0)
    d_bias_one = jnp.sum(first_normalized_gradient, axis=0)
    d_patches = grad_hidden + norm_gradient_step(
        first_normalized_gradient,
        first_centered_standard,
        first_inverse_spread,
        first_norm_gain.astype(jnp.float32),
    )
    a_gain, a_bias, a_qkv, a_qkvb, a_proj, a_projb = (
        lax.psum_scatter(first_gain_gradient, "shard", scatter_dimension=0, tiled=True),
        lax.psum_scatter(d_bias_one, "shard", scatter_dimension=0, tiled=True),
        lax.psum_scatter(d_w_qkv, "shard", scatter_dimension=0, tiled=True),
        lax.psum_scatter(d_b_qkv, "shard", scatter_dimension=0, tiled=True),
        lax.psum_scatter(d_w_proj, "shard", scatter_dimension=0, tiled=True),
        lax.psum_scatter(d_b_proj, "shard", scatter_dimension=0, tiled=True),
    )
    a_gain, a_bias, a_qkv, a_qkvb, a_proj, a_projb = lax.psum(
        (a_gain, a_bias, a_qkv, a_qkvb, a_proj, a_projb), "rep"
    )
    return (
        layer_out,
        d_patches,
        a_gain,
        a_bias,
        a_qkv,
        a_qkvb,
        a_proj,
        a_projb,
        m_gain,
        m_bias,
        m_up,
        m_upb,
        m_down,
        m_downb,
    )


def solution(mesh):
    in_specs = (
        P(("rep", "shard"), None),
        P(("rep", "shard"), None),
        P(None, ("rep", "shard")),
        P("shard"),
        P("shard"),
        P("shard", None),
        P("shard"),
        P("shard", None),
        P("shard"),
        P("shard"),
        P("shard"),
        P("shard", None),
        P("shard"),
        P("shard", None),
        P("shard"),
        P(("rep", "shard"), None),
    )
    out_specs = (
        P(("rep", "shard"), None),
        P(("rep", "shard"), None),
        P("shard"),
        P("shard"),
        P("shard", None),
        P("shard"),
        P("shard", None),
        P("shard"),
        P("shard"),
        P("shard"),
        P("shard", None),
        P("shard"),
        P("shard", None),
        P("shard"),
    )
    return jax.shard_map(
        per_device, mesh=mesh, in_specs=in_specs, out_specs=out_specs, check_vma=False
    )
```

profile of v0, /device:TPU:0, one launch (start us, length us, event | category | flops | bytes accessed | tf_op | source)
XLA Modules:
  0.0 2157.3 jit_solution(15266474193244514854)
XLA Ops:
  10.2 5.3 all-gather.4
  15.6 4.4 all-gather
  20.0 4.4 all-gather.5
  24.4 4.4 all-gather.1
  28.8 4.6 all-gather.3
  33.5 4.7 all-gather.2
  38.3 4.7 all-gather.6
  45.8 89.2 %all-gather.13.cloned.1.call-done = bf16[1280,3840]{1,0:T(8,128)(2,1)} async-done(((bf16[640,3840]{1,0:T(8,128)(2,1)}), bf16[1280,3840]{1,0:T(8,128)(2,1)}) %all-gather.13.cloned.1.call-update) | async-done | bytes 9830416 | tf_op jit(solution)/shard_map/all_gather | solution.py:136
  135.0 11.5 convolution_add_fusion
  146.6 9.2 copy.51
  155.8 3.3 slice_bitcast_fusion
  161.3 1.5 fusion.26
  162.9 7.7 fusion.51
  170.6 8.3 fusion
  178.9 10.5 fusion.32
  189.4 5.9 fusion.52
  195.7 147.2 %all-gather.17.cloned.1.call-done = bf16[1280,5120]{1,0:T(8,128)(2,1)} async-done(((bf16[640,5120]{1,0:T(8,128)(2,1)}), bf16[1280,5120]{1,0:T(8,128)(2,1)}) %all-gather.17.cloned.1.call-update) | async-done | bytes 13107216 | tf_op jit(solution)/shard_map/all_gather | solution.py:166
  342.9 13.6 fusion.47
  356.5 146.1 %all-gather.19.cloned.1.call-done = bf16[5120,1280]{1,0:T(8,128)(2,1)} async-done(((bf16[2560,1280]{1,0:T(8,128)(2,1)}), bf16[5120,1280]{1,0:T(8,128)(2,1)}) %all-gather.19.cloned.1.call-update) | async-done | bytes 13107216 | tf_op jit(solution)/shard_map/all_gather | solution.py:168
  502.6 16.9 convert_reduce_fusion
  519.4 15.0 multiply_reduce_fusion.1
  534.4 3.3 convert_reduce_fusion.4
  537.8 1.5 copy-done
  539.2 4.7 fusion.40
  544.0 5.7 convolution_convert_fusion
  549.7 2.9 copy.53
  552.5 12.1 multiply_reduce_fusion
  564.6 12.1 multiply_convert_fusion
  576.8 2.6 fusion.53
  579.5 1.7 bitcast_multiply_fusion.2
  583.9 8.7 fusion.29
  593.7 1.9 copy-done.9
  595.6 10.0 fusion.43
  605.7 15.4 fusion.48
  621.2 15.4 fusion.46
  637.3 12.7 fusion.21
  650.1 196.3 %reduce-scatter.5.cloned.1.call-done = f32[640,3840]{1,0:T(8,128)} async-done(((f32[1280,3840]{1,0:T(8,128)}), f32[640,3840]{1,0:T(8,128)}) %reduce-scatter.5.cloned.1.call-update) | async-done | bytes 9830416 | tf_op jit(solution)/shard_map/reduce_scatter | solution.py:261
  846.5 293.0 %reduce-scatter.11.cloned.1.call-done = f32[2560,1280]{1,0:T(8,128)} async-done(((f32[5120,1280]{1,0:T(8,128)}), f32[2560,1280]{1,0:T(8,128)}) %reduce-scatter.11.cloned.1.call-update) | async-done | bytes 13107216 | tf_op jit(solution)/shard_map/reduce_scatter | solution.py:217
  1139.5 293.0 %reduce-scatter.9.cloned.1.call-done = f32[640,5120]{1,0:T(8,128)} async-done(((f32[1280,5120]{1,0:T(8,128)}), f32[640,5120]{1,0:T(8,128)}) %reduce-scatter.9.cloned.1.call-update) | async-done | bytes 13107216 | tf_op jit(solution)/shard_map/reduce_scatter | solution.py:215
  1435.6 4.4 all-gather.7
  1440.1 5.3 fusion.20
  1445.4 15.7 fusion.14
  1467.3 63.9 %all-reduce.8 = (f32[640]{0:T(1024)}, f32[640]{0:T(1024)}, f32[1920]{0:T(1024)}, f32[640]{0:T(1024)}, f32[640]{0:T(1024)}, /*index=5*/f32[640]{0:T(1024)}, f32[2560]{0:T(1024)}, f32[640]{0:T(1024)}) all-reduce(f32[640]{0:T(1024)S(1)} %dynamic-slice.4, f32[640]{0:T(1024)S(1)} %dynamic-slice.6, ...), channel_id=1, replica_groups=mesh['rep'=16,'shard'=2] {'rep'}, use_global_device_ids=true, to_apply=%region_15.16 | all-reduce | flops 8320 | bytes 66560 | tf_op jit(solution)/shard_map/psum | solution.py:266
  1531.3 586.7 %all-reduce.14.cloned.1.call-done = (f32[640,3840]{1,0:T(8,128)}, f32[640,1280]{1,0:T(8,128)}, f32[640,5120]{1,0:T(8,128)}, f32[2560,1280]{1,0:T(8,128)}) async-done(((f32[640,3840]{1,0:T(8,128)}, f32[640,1280]{1,0:T(8,128)}, f32[640,5120]{1,0:T(8,128)}, f32[2560,1280]{1,0:T(8,128)}), (f32[640,3840]{1,0:T(8,128)}, f32[640,1280]{1,0:T(8,128)}, f32[640,5120]{1,0:T(8,128)}, ...) | async-done | bytes 39321616 | tf_op jit(solution)/shard_map/psum | solution.py:266
  2118.0 8.4 copy.73
  2126.5 1.7 copy.74
  2128.2 11.3 copy.75
  2139.5 10.5 copy.76
  (149 shorter events, 20.6 us)
Async XLA Ops:
  7.2 127.8 %all-gather.13.cloned.1.call-start = ((), (), s32[]{:S(2)}) async-start(), calls=%async_computation.4 | async-start | bytes 14745600 | tf_op jit(solution)/shard_map/all_gather | solution.py:136
  7.9 181.4 %all-gather.15.cloned.1.call-start = ((), (), s32[]{:S(2)}) async-start(), calls=%async_computation.5 | async-start | bytes 4915200 | tf_op jit(solution)/shard_map/all_gather | solution.py:138
  8.7 334.2 %all-gather.17.cloned.1.call-start = ((), (), s32[]{:S(2)}) async-start(), calls=%async_computation.6 | async-start | bytes 19660800 | tf_op jit(solution)/shard_map/all_gather | solution.py:166
  9.4 0.7 copy-start.25
  9.4 0.7 copy-start.26
  9.4 0.8 copy-start.27
  9.4 0.8 copy-start.28
  9.4 0.8 copy-start.29
  9.5 24.0 %copy-start.23 = (bf16[1920]{0:T(1024)(128)(2,1)S(1)}, bf16[1920]{0:T(1024)(128)(2,1)}, u32[]{:S(2)}) copy-start(bf16[1920]{0:T(1024)(128)(2,1)} %param.22) | copy-start | bytes 11524
  9.5 28.8 %copy-start.22 = (bf16[2560]{0:T(1024)(128)(2,1)S(1)}, bf16[2560]{0:T(1024)(128)(2,1)}, u32[]{:S(2)}) copy-start(bf16[2560]{0:T(1024)(128)(2,1)} %param.28) | copy-start | bytes 15364
  9.5 33.6 %copy-start.31 = (s32[1,4]{1,0:T(1,128)S(1)}, s32[1,4]{1,0:T(1,128)}, u32[]{:S(2)}) copy-start(s32[1,4]{1,0:T(1,128)} %param.17) | copy-start | bytes 52
  9.5 33.9 %copy-start.24 = (s32[2,512]{1,0:T(2,128)S(1)}, s32[2,512]{1,0:T(2,128)}, u32[]{:S(2)}) copy-start(s32[2,512]{1,0:T(2,128)} %param.18) | copy-start | bytes 12292
  9.5 35.3 %copy-start.1 = (bf16[512,1280]{1,0:T(8,128)(2,1)S(1)}, bf16[512,1280]{1,0:T(8,128)(2,1)}, u32[]{:S(2)}) copy-start(bf16[512,1280]{1,0:T(8,128)(2,1)} %param.16) | copy-start | bytes 3932164
  9.5 493.1 %all-gather.19.cloned.1.call-start = ((), (), s32[]{:S(2)}) async-start(), calls=%async_computation.7 | async-start | bytes 19660800 | tf_op jit(solution)/shard_map/all_gather | solution.py:168
  10.1 640.1 %reduce-scatter.7.cloned.1.call-start = ((), (), s32[]{:S(2)}) async-start(), calls=%async_computation.9 | async-start | bytes 9830400 | tf_op jit(solution)/shard_map/reduce_scatter | solution.py:263
  20.0 126.6 %copy-start.14 = (f32[1280]{0:T(1024)}, f32[1280]{0:T(1024)S(1)}, u32[]{:S(2)}) copy-start(f32[1280]{0:T(1024)S(1)} %reshape.326) | copy-start | bytes 15364
  28.8 117.7 %copy-start.20 = (f32[1280]{0:T(1024)}, f32[1280]{0:T(1024)S(1)}, u32[]{:S(2)}) copy-start(f32[1280]{0:T(1024)S(1)} %reshape.327) | copy-start | bytes 15364
  45.0 101.5 %copy-start.16 = (f32[512]{0:T(512)}, f32[512]{0:T(512)S(1)}, u32[]{:S(2)}) copy-start(f32[512]{0:T(512)S(1)} %broadcast_multiply_fusion.9) | copy-start | bytes 6148
  45.5 101.0 %copy-start.18 = (f32[512]{0:T(512)}, f32[512]{0:T(512)S(1)}, u32[]{:S(2)}) copy-start(f32[512]{0:T(512)S(1)} %add_rsqrt_fusion.1) | copy-start | bytes 6148
  155.8 4.3 slice-start
  159.2 2.1 slice-start.1
  162.9 7.7 copy-start.3
  162.9 7.7 copy-start.6
  519.4 15.0 copy-start.11
  534.4 4.8 copy-start.8
  537.8 1.5 copy-start
  543.9 302.6 %reduce-scatter.5.cloned.1.call-start = ((), (), s32[]{:S(2)}) async-start(), calls=%async_computation.8 | async-start | bytes 29491200 | tf_op jit(solution)/shard_map/reduce_scatter | solution.py:261
  564.6 12.1 copy-start.7
  576.8 2.6 copy-start.4
  576.8 2.6 copy-start.12
  581.4 0.9 copy-start.13
  582.4 1.5 copy-start.5
  592.6 3.0 copy-start.2
  592.6 3.0 copy-start.15
  592.6 3.0 copy-start.17
  592.6 3.0 copy-start.19
  592.7 3.0 copy-start.21
  593.7 1.9 copy-start.9
  605.7 533.8 %reduce-scatter.11.cloned.1.call-start = ((), (), s32[]{:S(2)}) async-start(), calls=%async_computation.11 | async-start | bytes 39321600 | tf_op jit(solution)/shard_map/reduce_scatter | solution.py:217
  621.1 811.3 %reduce-scatter.9.cloned.1.call-start = ((), (), s32[]{:S(2)}) async-start(), calls=%async_computation.10 | async-start | bytes 39321600 | tf_op jit(solution)/shard_map/reduce_scatter | solution.py:215
  636.6 824.6 %all-reduce.16.cloned.1.call-start = ((), (), s32[]{:S(2)}) async-start(), calls=%async_computation.13 | async-start | bytes 172032
  650.1 1468.0 %all-reduce.14.cloned.1.call-start = ((), (), s32[]{:S(2)}) async-start(), calls=%async_computation.12 | async-start | bytes 78643200 | tf_op jit(solution)/shard_map/psum | solution.py:266
  1432.4 0.7 copy-start.32
  1432.4 3.2 copy-start.30
  2118.0 8.5 copy-start.10
Sparse Core Ops, SparseCore 0:
  9.5 125.4 all-gather.12
  136.6 46.4 all-gather.14
  184.6 158.2 all-gather.16
  344.3 158.2 all-gather.18
  544.0 79.9 reduce-scatter.6
  626.2 220.1 reduce-scatter.4
  848.8 290.6 reduce-scatter.10
  1141.8 290.6 reduce-scatter.8
  1436.3 20.8 all-reduce.15
  1461.9 656.1 all-reduce.13
where the time goes:
time: 2170 us; the launch traced here: 2160 us
  waiting for transfers between devices  1750 us (81%)
  matrix products  186 us (9%)
  blocking collectives  101 us (5%)
  local copies, waits for them, and re-layouts  60.9 us (3%)
  other arithmetic  38 us (2%)
    psum x1, waiting for transfers between devices, per_device(): lax.psum((a_gain, a_bias, a_qkv, a_qkvb, a_proj, a_projb), 'rep')  587 us
    reduce_scatter x1, waiting for transfers between devices, per_device(): lax.psum_scatter(d_w_down, 'shard', scatter_dimension=0, tiled=True)  293 us
    reduce_scatter x1, waiting for transfers between devices, per_device(): lax.psum_scatter(d_w_up, 'shard', scatter_dimension=0, tiled=True)  293 us
    reduce_scatter x1, waiting for transfers between devices, per_device(): lax.psum_scatter(d_w_qkv, 'shard', scatter_dimension=0, tiled=True)  196 us
    all_gather x1, waiting for transfers between devices, per_device(): lax.all_gather(fc1_weight, 'shard', axis=0, tiled=True)  147 us
    all_gather x1, waiting for transfers between devices, per_device(): lax.all_gather(fc2_weight, 'shard', axis=0, tiled=True)  146 us
    all_gather x1, waiting for transfers between devices, per_device(): lax.all_gather(qkv_weight, 'shard', axis=0, tiled=True)  89.2 us
    psum x1, blocking collectives, per_device(): lax.psum((a_gain, a_bias, a_qkv, a_qkvb, a_proj, a_projb), 'rep')  63.9 us
  transfers between devices with their start and end apart: 10, of which 7 were waited for; matrix products, arithmetic and copies ran while one was open for 10% of the time, Pallas kernels for 0%

commit v1 on v0

--- a/solution.py
+++ b/solution.py
@@ -7,6 +7,23 @@
 HEADS = 16
 norm_eps = 1e-06
 quick_slope = 1.702
+
+
+def remake_wires(m):
+    built, aux, w_next = (lax.axis_size("shard"), lax.axis_index("shard"), m.shape[0])
+    z2, fresh = (m, 1)
+    while fresh < built:
+        z2 = jnp.concatenate(
+            [
+                z2,
+                lax.ppermute(
+                    z2, "shard", tuple(((at, (at - fresh) % built) for at in range(built)))
+                ),
+            ],
+            0,
+        )
+        fresh = 2 * fresh
+    return jnp.roll(z2, aux * w_next, 0)
 
 
 def apply_layer_norm(matrix):
@@ -163,7 +180,7 @@
     second_norm_gain, second_norm_bias, w_up, b_up, w_down, b_down = (
         lax.all_gather(ln2_gain, "shard", axis=0, tiled=True),
         lax.all_gather(ln2_bias, "shard", axis=0, tiled=True),
-        lax.all_gather(fc1_weight, "shard", axis=0, tiled=True),
+        remake_wires(fc1_weight),
         lax.all_gather(fc1_bias, "shard", axis=0, tiled=True),
         lax.all_gather(fc2_weight, "shard", axis=0, tiled=True),
         lax.all_gather(fc2_bias, "shard", axis=0, tiled=True),

time: 2170 us -> 2260 us (1.041)
  blocking collectives: 101 us -> 351 us
  waiting for transfers between devices: 1750 us -> 1590 us
    all_gather x1, blocking collectives: 4.6 us -> 255 us  [per_device(): lax.all_gather(proj_bias, 'shard', axis=0, tiled=True)]
    all_gather x1, waiting for transfers between devices: 89.2 us -> 0.01 us  [per_device(): lax.all_gather(qkv_weight, 'shard', axis=0, tiled=True)]
    all_gather x1, waiting for transfers between devices: 146 us -> 71.5 us  [per_device(): lax.all_gather(fc2_weight, 'shard', axis=0, tiled=True)]
  transfers between devices with their start and end apart: 10 -> 11, of which waited for: 7 -> 6; matrix products, arithmetic and copies ran while one was open for 10% -> 10% of each run, Pallas kernels for 0% -> 0%
where the time goes in v1:
time: 2260 us; the launch traced here: 2250 us
  waiting for transfers between devices  1590 us (70%)
  blocking collectives  351 us (16%)
  matrix products  197 us (9%)
  local copies, waits for them, and re-layouts  61.8 us (3%)
  other arithmetic  37.9 us (2%)
    psum x1, waiting for transfers between devices, per_device(): lax.psum((a_gain, a_bias, a_qkv, a_qkvb, a_proj, a_projb), 'rep')  587 us
    reduce_scatter x1, waiting for transfers between devices, per_device(): lax.psum_scatter(d_w_down, 'shard', scatter_dimension=0, tiled=True)  293 us
    reduce_scatter x1, waiting for transfers between devices, per_device(): lax.psum_scatter(d_w_up, 'shard', scatter_dimension=0, tiled=True)  293 us
    all_gather x1, blocking collectives, per_device(): lax.all_gather(proj_bias, 'shard', axis=0, tiled=True)  255 us
    reduce_scatter x1, waiting for transfers between devices, per_device(): lax.psum_scatter(d_w_qkv, 'shard', scatter_dimension=0, tiled=True)  196 us
    all_gather x1, waiting for transfers between devices, per_device(): lax.all_gather(fc1_weight, 'shard', axis=0, tiled=True)  143 us
    all_gather x1, waiting for transfers between devices, per_device(): lax.all_gather(fc2_weight, 'shard', axis=0, tiled=True)  71.5 us
    psum x1, blocking collectives, per_device(): lax.psum((a_gain, a_bias, a_qkv, a_qkvb, a_proj, a_projb), 'rep')  63.9 us
  transfers between devices with their start and end apart: 11, of which 6 were waited for; matrix products, arithmetic and copies ran while one was open for 10% of the time, Pallas kernels for 0%

profile of v1, /device:TPU:0, one launch (start us, length us, event | category | flops | bytes accessed | tf_op | source)
XLA Modules:
  0.0 2254.3 jit_solution(1124208430337465535)
XLA Ops:
  9.5 3.1 collective-permute-start
  12.7 255.3 %all-gather.3 = bf16[2,1,640]{2,1,0:T(2,128)(2,1)S(1)} all-gather(bf16[1,1,640]{2,1,0:T(2,128)(2,1)S(1)} %reshape.316), channel_id=1, replica_groups=mesh['rep'=16,'shard'=2] {'shard'}, dimensions={0}, use_global_device_ids=true | all-gather | bytes 3840 | tf_op jit(solution)/shard_map/all_gather | solution.py:156
  268.1 5.0 all-gather.2
  273.1 4.5 all-gather.1
  277.8 4.5 all-gather
  283.7 4.5 all-gather.5
  288.3 4.5 all-gather.4
  292.9 4.4 all-gather.6
  298.7 12.1 convolution_add_fusion
  310.8 9.6 copy.51
  320.5 3.8 slice_bitcast_fusion
  326.5 1.5 fusion.31
  328.0 7.7 fusion.57
  335.7 8.3 fusion
  344.0 10.5 fusion.37
  354.5 4.8 fusion.58
  359.7 25.3 %fusion.4 = f32[512,5120]{1,0:T(8,128)} fusion(s32[]{:T(128)S(6)} %select_n.22, bf16[640,5120]{1,0:T(8,128)(2,1)} %param.27, bf16[640,5120]{1,0:T(8,128)(2,1)} %collective-permute-done, f32[512,1280]{1,0:T(8,128)S(1)} %get-tuple-element.125, f32[1280]{0:T(1024)S(1)} %reshape.331, f32[1280]{0:T(1024)S(1)} %reshape.330, f32[512]{0:T(512)S(1)} %add_rsqrt_fusion, ...), kind=kOutput, calls=%fused_computation.14 | convolution fusion | flops 6766592000 | bytes 26228740 | tf_op jit(solution)/shard_map/dot_general | solution.py:193
  385.0 71.5 %all-gather.17.cloned.1.call-done = bf16[5120,1280]{1,0:T(8,128)(2,1)} async-done(((bf16[2560,1280]{1,0:T(8,128)(2,1)}), bf16[5120,1280]{1,0:T(8,128)(2,1)}) %all-gather.17.cloned.1.call-update) | async-done | bytes 13107216 | tf_op jit(solution)/shard_map/all_gather | solution.py:185
  456.5 16.5 convert_reduce_fusion
  472.9 143.2 %all-gather.19.cloned.1.call-done = bf16[1280,5120]{1,0:T(8,128)(2,1)} async-done(((bf16[640,5120]{1,0:T(8,128)(2,1)}), bf16[1280,5120]{1,0:T(8,128)(2,1)}) %all-gather.19.cloned.1.call-update) | async-done | bytes 13107216 | tf_op jit(solution)/shard_map/all_gather | solution.py:207
  616.2 15.3 multiply_reduce_fusion.1
  631.5 3.3 convert_reduce_fusion.4
  634.8 1.5 copy-done
  636.3 4.7 fusion.47
  641.1 5.7 convolution_convert_fusion
  646.8 2.9 copy.53
  649.6 12.1 multiply_reduce_fusion
  661.7 12.1 multiply_convert_fusion
  673.9 2.6 fusion.59
  676.5 1.7 bitcast_multiply_fusion.2
  680.9 8.7 fusion.34
  690.8 1.9 copy-done.9
  692.7 10.0 fusion.50
  702.8 15.4 fusion.54
  718.3 15.4 fusion.53
  734.4 12.7 fusion.26
  747.2 196.3 %reduce-scatter.5.cloned.1.call-done = f32[640,3840]{1,0:T(8,128)} async-done(((f32[1280,3840]{1,0:T(8,128)}), f32[640,3840]{1,0:T(8,128)}) %reduce-scatter.5.cloned.1.call-update) | async-done | bytes 9830416 | tf_op jit(solution)/shard_map/reduce_scatter | solution.py:278
  943.6 293.0 %reduce-scatter.11.cloned.1.call-done = f32[2560,1280]{1,0:T(8,128)} async-done(((f32[5120,1280]{1,0:T(8,128)}), f32[2560,1280]{1,0:T(8,128)}) %reduce-scatter.11.cloned.1.call-update) | async-done | bytes 13107216 | tf_op jit(solution)/shard_map/reduce_scatter | solution.py:234
  1236.5 293.0 %reduce-scatter.9.cloned.1.call-done = f32[640,5120]{1,0:T(8,128)} async-done(((f32[1280,5120]{1,0:T(8,128)}), f32[640,5120]{1,0:T(8,128)}) %reduce-scatter.9.cloned.1.call-update) | async-done | bytes 13107216 | tf_op jit(solution)/shard_map/reduce_scatter | solution.py:232
  1530.2 4.4 all-gather.7
  1537.2 5.3 fusion.25
  1542.5 15.7 fusion.19
  1564.5 63.9 %all-reduce.8 = (f32[640]{0:T(1024)}, f32[640]{0:T(1024)}, f32[1920]{0:T(1024)}, f32[640]{0:T(1024)}, f32[640]{0:T(1024)}, /*index=5*/f32[640]{0:T(1024)}, f32[2560]{0:T(1024)}, f32[640]{0:T(1024)}) all-reduce(f32[640]{0:T(1024)S(1)} %dynamic-slice.4, f32[640]{0:T(1024)S(1)} %dynamic-slice.6, ...), channel_id=1, replica_groups=mesh['rep'=16,'shard'=2] {'rep'}, use_global_device_ids=true, to_apply=%region_15.16 | all-reduce | flops 8320 | bytes 66560 | tf_op jit(solution)/shard_map/psum | solution.py:283
  1628.4 586.7 %all-reduce.14.cloned.1.call-done = (f32[640,3840]{1,0:T(8,128)}, f32[640,1280]{1,0:T(8,128)}, f32[640,5120]{1,0:T(8,128)}, f32[2560,1280]{1,0:T(8,128)}) async-done(((f32[640,3840]{1,0:T(8,128)}, f32[640,1280]{1,0:T(8,128)}, f32[640,5120]{1,0:T(8,128)}, f32[2560,1280]{1,0:T(8,128)}), (f32[640,3840]{1,0:T(8,128)}, f32[640,1280]{1,0:T(8,128)}, f32[640,5120]{1,0:T(8,128)}, ...) | async-done | bytes 39321616 | tf_op jit(solution)/shard_map/psum | solution.py:283
  2215.1 8.4 copy.73
  2223.6 1.7 copy.74
  2225.3 11.3 copy.75
  2236.5 10.5 copy.76
  (151 shorter events, 20.1 us)
Async XLA Ops:
  7.2 291.6 %all-gather.13.cloned.1.call-start = ((), (), s32[]{:S(2)}) async-start(), calls=%async_computation.4 | async-start | bytes 14745600 | tf_op jit(solution)/shard_map/all_gather | solution.py:153
  7.9 346.6 %all-gather.15.cloned.1.call-start = ((), (), s32[]{:S(2)}) async-start(), calls=%async_computation.5 | async-start | bytes 4915200 | tf_op jit(solution)/shard_map/all_gather | solution.py:155
  8.7 447.8 %all-gather.17.cloned.1.call-start = ((), (), s32[]{:S(2)}) async-start(), calls=%async_computation.6 | async-start | bytes 19660800 | tf_op jit(solution)/shard_map/all_gather | solution.py:185
  9.4 3.3 copy-start.25
  9.4 258.7 %copy-start.23 = (bf16[1920]{0:T(1024)(128)(2,1)S(1)}, bf16[1920]{0:T(1024)(128)(2,1)}, u32[]{:S(2)}) copy-start(bf16[1920]{0:T(1024)(128)(2,1)} %param.22) | copy-start | bytes 11524
  9.4 263.7 %copy-start.26 = (bf16[640]{0:T(1024)(128)(2,1)S(1)}, bf16[640]{0:T(1024)(128)(2,1)}, u32[]{:S(2)}) copy-start(bf16[640]{0:T(1024)(128)(2,1)} %param.20) | copy-start | bytes 3844
  9.4 268.3 %copy-start.27 = (bf16[640]{0:T(1024)(128)(2,1)S(1)}, bf16[640]{0:T(1024)(128)(2,1)}, u32[]{:S(2)}) copy-start(bf16[640]{0:T(1024)(128)(2,1)} %param.19) | copy-start | bytes 3844
  9.4 272.9 %copy-start.1 = (bf16[512,1280]{1,0:T(8,128)(2,1)S(1)}, bf16[512,1280]{1,0:T(8,128)(2,1)}, u32[]{:S(2)}) copy-start(bf16[512,1280]{1,0:T(8,128)(2,1)} %param.16) | copy-start | bytes 3932164
  9.5 606.7 %all-gather.19.cloned.1.call-start = ((), (), s32[]{:S(2)}) async-start(), calls=%async_computation.7 | async-start | bytes 19660800 | tf_op jit(solution)/shard_map/all_gather | solution.py:207
  9.5 350.2 %collective-permute-start = (bf16[640,5120]{1,0:T(8,128)(2,1)}, bf16[640,5120]{1,0:T(8,128)(2,1)}, u32[]{:S(2)}, u32[]{:S(2)}) collective-permute-start(bf16[640,5120]{1,0:T(8,128)(2,1)} %param.27), channel_id=1, source_target_pairs={{0,1},{1,0},{2,3},{3,2},{4,5},{5,4},{6,7},{7,6},{8,9},{9,8},{10,11... | collective-permute-start | bytes 19660808 | tf_op jit(solution)/shard_map/ppermute | solution.py:19
  12.6 270.5 %copy-start.24 = (s32[2,512]{1,0:T(2,128)S(1)}, s32[2,512]{1,0:T(2,128)}, u32[]{:S(2)}) copy-start(s32[2,512]{1,0:T(2,128)} %param.18) | copy-start | bytes 12292
  12.6 270.6 %copy-start.31 = (s32[1,4]{1,0:T(1,128)S(1)}, s32[1,4]{1,0:T(1,128)}, u32[]{:S(2)}) copy-start(s32[1,4]{1,0:T(1,128)} %param.17) | copy-start | bytes 52
  12.6 271.1 %copy-start.28 = (bf16[640]{0:T(1024)(128)(2,1)S(1)}, bf16[640]{0:T(1024)(128)(2,1)}, u32[]{:S(2)}) copy-start(bf16[640]{0:T(1024)(128)(2,1)} %param.26) | copy-start | bytes 3844
  12.6 275.7 %copy-start.29 = (bf16[640]{0:T(1024)(128)(2,1)S(1)}, bf16[640]{0:T(1024)(128)(2,1)}, u32[]{:S(2)}) copy-start(bf16[640]{0:T(1024)(128)(2,1)} %param.25) | copy-start | bytes 3844
  12.6 280.3 %copy-start.22 = (bf16[2560]{0:T(1024)(128)(2,1)S(1)}, bf16[2560]{0:T(1024)(128)(2,1)}, u32[]{:S(2)}) copy-start(bf16[2560]{0:T(1024)(128)(2,1)} %param.28) | copy-start | bytes 15364
  12.6 734.6 %reduce-scatter.7.cloned.1.call-start = ((), (), s32[]{:S(2)}) async-start(), calls=%async_computation.9 | async-start | bytes 9830400 | tf_op jit(solution)/shard_map/reduce_scatter | solution.py:280
  277.7 33.1 %copy-start.20 = (f32[1280]{0:T(1024)}, f32[1280]{0:T(1024)S(1)}, u32[]{:S(2)}) copy-start(f32[1280]{0:T(1024)S(1)} %reshape.327) | copy-start | bytes 15364
  282.4 28.5 %copy-start.14 = (f32[1280]{0:T(1024)}, f32[1280]{0:T(1024)S(1)}, u32[]{:S(2)}) copy-start(f32[1280]{0:T(1024)S(1)} %reshape.326) | copy-start | bytes 15364
  282.6 28.2 %copy-start.16 = (f32[512]{0:T(512)}, f32[512]{0:T(512)S(1)}, u32[]{:S(2)}) copy-start(f32[512]{0:T(512)S(1)} %broadcast_multiply_fusion.9) | copy-start | bytes 6148
  283.1 27.7 %copy-start.18 = (f32[512]{0:T(512)}, f32[512]{0:T(512)S(1)}, u32[]{:S(2)}) copy-start(f32[512]{0:T(512)S(1)} %add_rsqrt_fusion.1) | copy-start | bytes 6148
  320.5 4.7 slice-start
  324.3 2.2 slice-start.1
  328.0 7.7 copy-start.3
  328.0 7.7 copy-start.6
  616.2 15.3 copy-start.11
  631.5 4.8 copy-start.8
  634.8 1.5 copy-start
  641.0 302.5 %reduce-scatter.5.cloned.1.call-start = ((), (), s32[]{:S(2)}) async-start(), calls=%async_computation.8 | async-start | bytes 29491200 | tf_op jit(solution)/shard_map/reduce_scatter | solution.py:278
  661.7 12.1 copy-start.7
  673.9 2.6 copy-start.4
  673.9 2.6 copy-start.12
  678.5 0.9 copy-start.13
  679.5 1.5 copy-start.5
  689.7 3.0 copy-start.2
  689.7 3.0 copy-start.15
  689.7 3.0 copy-start.17
  689.7 3.0 copy-start.19
  689.7 3.0 copy-start.21
  690.8 1.9 copy-start.9
  702.7 533.8 %reduce-scatter.11.cloned.1.call-start = ((), (), s32[]{:S(2)}) async-start(), calls=%async_computation.11 | async-start | bytes 39321600 | tf_op jit(solution)/shard_map/reduce_scatter | solution.py:234
  718.2 811.3 %reduce-scatter.9.cloned.1.call-start = ((), (), s32[]{:S(2)}) async-start(), calls=%async_computation.10 | async-start | bytes 39321600 | tf_op jit(solution)/shard_map/reduce_scatter | solution.py:232
  733.7 824.6 %all-reduce.16.cloned.1.call-start = ((), (), s32[]{:S(2)}) async-start(), calls=%async_computation.13 | async-start | bytes 172032
  747.2 1468.0 %all-reduce.14.cloned.1.call-start = ((), (), s32[]{:S(2)}) async-start(), calls=%async_computation.12 | async-start | bytes 78643200 | tf_op jit(solution)/shard_map/psum | solution.py:283
  1529.5 0.7 copy-start.30
  1529.5 5.1 copy-start.32
  2215.1 8.5 copy-start.10
Sparse Core Ops, SparseCore 0:
  9.5 230.4 all-gather.12
  241.6 53.5 all-gather.14
  296.7 159.7 all-gather.16
  457.9 158.2 all-gather.18
  641.1 79.9 reduce-scatter.6
  723.3 220.2 reduce-scatter.4
  945.9 290.6 reduce-scatter.10
  1238.8 290.6 reduce-scatter.8
  1533.4 20.8 all-reduce.15
  1559.0 656.1 all-reduce.13
